TPU v7x, 32 devices: a whole 2x2x4 slice. The times are simulated.
32 devices in a mesh: section: 4 (over y, x), dp: 2 (over core), tensor: 4 (over z).
Axes of the slice: x: 2, y: 2, z: 4, core: 2. Of those that a mesh axis runs over, the one named last changes fastest.
Arguments:
- cotangent: bfloat16 [2, 256, 8192], P(None, 'dp', 'tensor'), may hold values from -6 to 6
- stash: bfloat16 [4, 2, 256, 8192], P('section', None, 'dp', 'tensor'), may hold values from -0.25 to 0.25
- factor_a: bfloat16 [4, 1024, 8192], P('section', 'dp', 'tensor'), may hold values from -0.0625 to 0.0625
- factor_b: bfloat16 [4, 8192, 1024], P('section', ('tensor', 'dp')), may hold values from -0.1875 to 0.1875
- block_vals: bfloat16 [4, 8, 128, 128], P('section', ('dp', 'tensor')), may hold values from -0.25 to 0.25
- block_rows: int32 [4, 8], P('section'), may hold values from 0 to 63, as said below
- block_cols: int32 [4, 8], P('section'), may hold values from 0 to 63, as said below
Outputs:
- grad_in: bfloat16 [4, 2, 256, 8192], P('section', None, 'dp', 'tensor')
- block_grad: float32 [4, 8, 128, 128], P('section', ('dp', 'tensor'))
Inputs may be any that keep to these rules, and one draw needn't show every extreme that they name: The support lies inside the diagonal part of each tensor shard. Within a section all (block_rows, block_cols) pairs are distinct. For every dp index o < 2, tensor index t < 4 and slot k < 1, the block at position (o * 4 + t) + k has both its row and its column block index in [t * 8192 // (128 * 4), (t + 1) * 8192 // (128 * 4)). `block_cols`: drawn together with block_rows; the same promise holds.
All inputs are finite; a program needn't handle non-finite values.
Results may differ from a plain program's by a relative error of at most 0.024.
Values may be sent and summed in bfloat16 or wider, within the bound.
A program may use at most 128 MiB of HBM per device.

v0:
```python
import jax
import jax.numpy as jnp
from jax import lax
from jax.sharding import PartitionSpec as P


def shifted(value, axis, steps):
    count = lax.axis_size(axis)
    initial, last = (max(0, -steps), min(count, count - steps))
    return lax.ppermute(value, axis, [(source, source + steps) for source in range(initial, last)])


def pass_back(grad_out):
    return shifted(grad_out, "section", -1)


def on_device(cotangent, stash, factor_a, factor_b, block_vals, block_rows, block_cols):
    sections = lax.axis_size("section")
    section_pos = lax.axis_index("section")
    tensor_pos = lax.axis_index("tensor")
    dp_count = lax.axis_size("dp")
    tensor_count = lax.axis_size("tensor")
    left_full, right_full, values = (
        lax.all_gather(factor_a[0], "dp", axis=0, tiled=True),
        lax.all_gather(factor_b[0], "dp", axis=0, tiled=True),
        lax.all_gather(block_vals[0], "dp", axis=0, tiled=True),
    )
    batches = stash.shape[1]
    tokens_here = stash.shape[2]
    local_width = stash.shape[3]
    block_size = block_vals.shape[-1]
    local_blocks = local_width // block_size

    def local_ids(table):
        grid = table[0].reshape(dp_count, tensor_count, -1)
        mine = lax.dynamic_index_in_dim(grid, tensor_pos, 1, keepdims=False)
        return mine.reshape(-1) - tensor_pos * local_blocks

    positions = jnp.arange(local_blocks, dtype=jnp.int32)[None, :]
    row_hits = local_ids(block_rows)[:, None] == positions
    col_hits = local_ids(block_cols)[:, None] == positions
    row_pick = row_hits.astype(jnp.bfloat16)
    row_double = jnp.concatenate([row_pick, row_pick], axis=0)
    col_pick = col_hits.astype(jnp.bfloat16)
    grad_sum = jnp.zeros((values.shape[0], block_size, block_size), jnp.float32)
    grads_in = jnp.zeros(stash.shape[1:], jnp.bfloat16)
    received = jnp.zeros((tokens_here, local_width), jnp.bfloat16)
    steps = batches + sections - 1
    for step_idx in range(steps):
        batch_pos = step_idx - (sections - 1 - section_pos)
        active = (batch_pos >= 0) & (batch_pos < batches)
        slot_pos = jnp.clip(batch_pos, 0, batches - 1)
        fresh = lax.dynamic_index_in_dim(cotangent, slot_pos, 0, keepdims=False)
        cot_now = jnp.where(section_pos == sections - 1, fresh, received)
        partial_value = jnp.einsum(
            "td,rd->tr", cot_now, left_full, preferred_element_type=jnp.float32
        )
        share = lax.psum_scatter(
            partial_value.astype(jnp.bfloat16), "tensor", scatter_dimension=1, tiled=True
        )
        rank_act = lax.all_gather(share, "tensor", axis=1, tiled=True)
        picked_cot = jnp.einsum(
            "tlc,nl->tnc",
            cot_now.reshape(tokens_here, local_blocks, block_size),
            col_pick,
            preferred_element_type=jnp.float32,
        ).astype(jnp.bfloat16)
        sparse_terms = jnp.einsum(
            "tnc,nrc->tnr", picked_cot, values, preferred_element_type=jnp.float32
        )
        upper_part = sparse_terms.astype(jnp.bfloat16)
        lower_part = (sparse_terms - upper_part.astype(jnp.float32)).astype(jnp.bfloat16)
        both_parts = jnp.concatenate([upper_part, lower_part], axis=1)
        sparse_grad = jnp.einsum(
            "tnr,nl->tlr", both_parts, row_double, preferred_element_type=jnp.float32
        )
        dense_grad = jnp.einsum(
            "tr,dr->td", rank_act, right_full, preferred_element_type=jnp.float32
        )
        grad_out = (dense_grad + sparse_grad.reshape(tokens_here, local_width)).astype(jnp.bfloat16)
        current = lax.dynamic_index_in_dim(grads_in, slot_pos, 0, keepdims=False)
        grads_in = lax.dynamic_update_index_in_dim(
            grads_in, jnp.where(active, grad_out, current), slot_pos, 0
        )
        stash_now = lax.dynamic_index_in_dim(stash[0], slot_pos, 0, keepdims=False)
        live_scale = active.astype(jnp.bfloat16)
        if step_idx + 1 < steps:
            received = pass_back(grad_out)
        picked_in = (
            jnp.einsum(
                "tlr,nl->tnr",
                stash_now.reshape(tokens_here, local_blocks, block_size),
                row_pick,
                preferred_element_type=jnp.float32,
            ).astype(jnp.bfloat16)
            * live_scale
        )
        grad_sum = grad_sum + jnp.einsum(
            "tnr,tnc->nrc", picked_in, picked_cot, preferred_element_type=jnp.float32
        )
    block_grad = lax.psum_scatter(
        grad_sum.astype(jnp.bfloat16), "dp", scatter_dimension=0, tiled=True
    ).astype(jnp.float32)
    return (grads_in[None], block_grad[None])


def solution(mesh):
    in_specs = (
        P(None, "dp", "tensor"),
        P("section", None, "dp", "tensor"),
        P("section", "dp", "tensor"),
        P("section", ("tensor", "dp"), None),
        P("section", ("dp", "tensor"), None, None),
        P("section", None),
        P("section", None),
    )
    out_specs = (P("section", None, "dp", "tensor"), P("section", ("dp", "tensor"), None, None))
    return jax.shard_map(
        on_device, mesh=mesh, in_specs=in_specs, out_specs=out_specs, check_vma=False
    )
```

profile of v0, /device:TPU:0, one launch (start us, length us, event | category | flops | bytes accessed | tf_op | source)
XLA Modules:
  0.0 300.2 jit_solution(10202126768568250833)
XLA Ops:
  8.0 17.9 %all-gather.6.cloned.1.call-done = bf16[1,1024,2048]{2,1,0:T(8,128)(2,1)} async-done(((bf16[1,512,2048]{2,1,0:T(8,128)(2,1)}), bf16[1,1024,2048]{2,1,0:T(8,128)(2,1)}) %all-gather.6.cloned.1.call-update) | async-done | bytes 4194320 | tf_op jit(solution)/shard_map/all_gather | solution.py:24
  25.9 4.6 %fusion.59 = bf16[128,1024]{1,0:T(8,128)(2,1)} fusion(bf16[1,1024,2048]{2,1,0:T(8,128)(2,1)} %all-gather.6.cloned.1.call-done, bf16[2,128,2048]{2,1,0:T(8,128)(2,1)} %param.7, s32[]{:T(128)S(6)} %min.16, pred[]{:T(512)S(6)} %eq.14), kind=kOutput, calls=%fused_computation.33 | convolution fusion | flops 537264128 | bytes 4980741 | tf_op jit(solution)/shard_map/td,rd->tr/dot_general | solution.py:55
  33.6 1.5 dynamic-slice_bitcast_fusion
  35.0 0.9 copy.71
  36.2 1.9 all-gather.2
  39.0 12.9 %reduce-scatter.7.cloned.1.call-done = bf16[128,256]{1,0:T(8,128)(2,1)} async-done(((bf16[128,1024]{1,0:T(8,128)(2,1)}), bf16[128,256]{1,0:T(8,128)(2,1)}) %reduce-scatter.7.cloned.1.call-update) | async-done | bytes 65552 | tf_op jit(solution)/shard_map/reduce_scatter | solution.py:58
  51.9 14.0 %all_gather.25 = bf16[128,1024]{1,0:T(8,128)(2,1)S(1)} all-gather(bf16[128,256]{1,0:T(8,128)(2,1)} %reduce-scatter.7.cloned.1.call-done), channel_id=1, replica_groups=mesh['section'=4,'dp'=2,'tensor'=4] {'tensor'}, dimensions={1}, use_global_device_ids=true | all-gather | bytes 327680 | tf_op jit(solution)/shard_map/all_gather | solution.py:61
  66.0 4.7 %bitcast_dynamic-update-slice_fusion.3 = (bf16[2,128,2048]{2,1,0:T(8,128)(2,1)S(1)}, bf16[128,2048]{1,0:T(8,128)(2,1)}) fusion(bf16[2,128,2048]{2,1,0:T(8,128)(2,1)S(1)} %broadcast_in_dim.36, s32[]{:T(128)S(6)} %min.16, pred[]{:T(512)S(6)} %and.17, f32[16,8,16,128]{3,2,1,0:T(8,128)S(1)} %bitcast.277, bf16[128,1024]{1,0:T(8,128)(2,1)S(1)} %all_gather.25, ...), kind=kOutput, calls=%fused_computation.83 | convolution fusion | flops 537657344 | bytes 6553605 | tf_op jit(solution)/shard_map/tr,dr->td/dot_general | solution.py:77
  70.7 1.3 collective-permute-start
  72.0 2.0 fusion.81
  74.0 1.1 copy.72
  75.1 2.0 copy.73
  77.1 0.9 fusion.83
  78.8 7.5 %collective-permute-done = bf16[128,2048]{1,0:T(8,128)(2,1)S(1)} collective-permute-done((bf16[128,2048]{1,0:T(8,128)(2,1)}, bf16[128,2048]{1,0:T(8,128)(2,1)S(1)}, u32[]{:S(2)}, u32[]{:S(2)}) %collective-permute-start) | collective-permute-done | bytes 524320 | tf_op jit(solution)/shard_map/ppermute | solution.py:10
  86.8 2.2 fusion.62
  89.8 20.7 %reduce-scatter.9.cloned.1.call-done = bf16[128,256]{1,0:T(8,128)(2,1)} async-done(((bf16[128,1024]{1,0:T(8,128)(2,1)}), bf16[128,256]{1,0:T(8,128)(2,1)}) %reduce-scatter.9.cloned.1.call-update) | async-done | bytes 65552 | tf_op jit(solution)/shard_map/reduce_scatter | solution.py:58
  110.4 14.2 %all_gather.28 = bf16[128,1024]{1,0:T(8,128)(2,1)S(1)} all-gather(bf16[128,256]{1,0:T(8,128)(2,1)} %reduce-scatter.9.cloned.1.call-done), channel_id=1, replica_groups=mesh['section'=4,'dp'=2,'tensor'=4] {'tensor'}, dimensions={1}, use_global_device_ids=true | all-gather | bytes 327680 | tf_op jit(solution)/shard_map/all_gather | solution.py:61
  124.6 4.8 %bitcast_dynamic-update-slice_fusion.2 = (bf16[2,128,2048]{2,1,0:T(8,128)(2,1)S(1)}, bf16[128,2048]{1,0:T(8,128)(2,1)}) fusion(bf16[2,128,2048]{2,1,0:T(8,128)(2,1)S(1)} %get-tuple-element.17, s32[]{:T(128)S(6)} %min.17, bf16[1,128,2048]{2,1,0:T(8,128)(2,1)} %constant_dynamic-slice_fusion.2, pred[]{:T(512)S(6)} %and.18, ...), kind=kOutput, calls=%fused_computation.80 | convolution fusion | flops 537657344 | bytes 7077893 | tf_op jit(solution)/shard_map/tr,dr->td/dot_general | solution.py:77
  129.4 1.3 collective-permute-start.1
  130.7 0.9 fusion.85
  131.6 1.1 copy.74
  132.8 0.9 fusion.87
  133.7 0.8 constant_dynamic-slice_fusion.1
  134.6 6.4 %collective-permute-done.1 = bf16[128,2048]{1,0:T(8,128)(2,1)S(1)} collective-permute-done((bf16[128,2048]{1,0:T(8,128)(2,1)}, bf16[128,2048]{1,0:T(8,128)(2,1)S(1)}, u32[]{:S(2)}, u32[]{:S(2)}) %collective-permute-start.1) | collective-permute-done | bytes 524320 | tf_op jit(solution)/shard_map/ppermute | solution.py:10
  141.4 2.2 fusion.65
  144.4 17.8 %reduce-scatter.11.cloned.1.call-done = bf16[128,256]{1,0:T(8,128)(2,1)} async-done(((bf16[128,1024]{1,0:T(8,128)(2,1)}), bf16[128,256]{1,0:T(8,128)(2,1)}) %reduce-scatter.11.cloned.1.call-update) | async-done | bytes 65552 | tf_op jit(solution)/shard_map/reduce_scatter | solution.py:58
  162.2 14.4 %all_gather.29 = bf16[128,1024]{1,0:T(8,128)(2,1)S(1)} all-gather(bf16[128,256]{1,0:T(8,128)(2,1)} %reduce-scatter.11.cloned.1.call-done), channel_id=1, replica_groups=mesh['section'=4,'dp'=2,'tensor'=4] {'tensor'}, dimensions={1}, use_global_device_ids=true | all-gather | bytes 327680 | tf_op jit(solution)/shard_map/all_gather | solution.py:61
  176.6 4.8 %bitcast_dynamic-update-slice_fusion.1 = (bf16[2,128,2048]{2,1,0:T(8,128)(2,1)S(1)}, bf16[128,2048]{1,0:T(8,128)(2,1)}) fusion(bf16[2,128,2048]{2,1,0:T(8,128)(2,1)S(1)} %get-tuple-element.19, s32[]{:T(128)S(6)} %min.18, bf16[1,128,2048]{2,1,0:T(8,128)(2,1)} %constant_dynamic-slice_fusion.1, pred[]{:T(512)S(6)} %and.19, ...), kind=kOutput, calls=%fused_computation.77 | convolution fusion | flops 537657344 | bytes 7077893 | tf_op jit(solution)/shard_map/tr,dr->td/dot_general | solution.py:77
  181.4 1.3 collective-permute-start.2
  182.7 0.9 fusion.116
  183.6 1.1 copy.75
  184.7 0.9 fusion.89
  185.6 0.9 constant_dynamic-slice_fusion
  186.6 6.2 %collective-permute-done.2 = bf16[128,2048]{1,0:T(8,128)(2,1)S(1)} collective-permute-done((bf16[128,2048]{1,0:T(8,128)(2,1)}, bf16[128,2048]{1,0:T(8,128)(2,1)S(1)}, u32[]{:S(2)}, u32[]{:S(2)}) %collective-permute-start.2) | collective-permute-done | bytes 524320 | tf_op jit(solution)/shard_map/ppermute | solution.py:10
  193.2 2.2 fusion.68
  196.2 17.9 %reduce-scatter.13.cloned.1.call-done = bf16[128,256]{1,0:T(8,128)(2,1)} async-done(((bf16[128,1024]{1,0:T(8,128)(2,1)}), bf16[128,256]{1,0:T(8,128)(2,1)}) %reduce-scatter.13.cloned.1.call-update) | async-done | bytes 65552 | tf_op jit(solution)/shard_map/reduce_scatter | solution.py:58
  214.0 14.2 %all_gather.30 = bf16[128,1024]{1,0:T(8,128)(2,1)S(1)} all-gather(bf16[128,256]{1,0:T(8,128)(2,1)} %reduce-scatter.13.cloned.1.call-done), channel_id=1, replica_groups=mesh['section'=4,'dp'=2,'tensor'=4] {'tensor'}, dimensions={1}, use_global_device_ids=true | all-gather | bytes 327680 | tf_op jit(solution)/shard_map/all_gather | solution.py:61
  228.2 4.0 %bitcast_dynamic-update-slice_fusion = (bf16[2,128,2048]{2,1,0:T(8,128)(2,1)S(1)}, bf16[128,2048]{1,0:T(8,128)(2,1)S(1)}) fusion(bf16[2,128,2048]{2,1,0:T(8,128)(2,1)S(1)} %get-tuple-element.21, s32[]{:T(128)S(6)} %min.19, bf16[1,128,2048]{2,1,0:T(8,128)(2,1)} %constant_dynamic-slice_fusion, pred[]{:T(512)S(6)} %and.20, ...), kind=kOutput, calls=%fused_computation.74 | convolution fusion | flops 537657344 | bytes 7077893 | tf_op jit(solution)/shard_map/tr,dr->td/dot_general | solution.py:77
  232.3 1.4 collective-permute-start.3
  234.4 1.0 copy.135
  235.3 8.4 %collective-permute-done.3 = bf16[128,2048]{1,0:T(8,128)(2,1)S(1)} collective-permute-done((bf16[128,2048]{1,0:T(8,128)(2,1)S(1)}, bf16[128,2048]{1,0:T(8,128)(2,1)S(1)}, u32[]{:S(2)}, u32[]{:S(2)}) %collective-permute-start.3) | collective-permute-done | bytes 524320 | tf_op jit(solution)/shard_map/ppermute | solution.py:10
  244.2 0.9 fusion.74
  245.1 4.4 %fusion.71 = bf16[128,1024]{1,0:T(8,128)(2,1)} fusion(bf16[1,1024,2048]{2,1,0:T(8,128)(2,1)} %all-gather.6.cloned.1.call-done, bf16[128,2048]{1,0:T(8,128)(2,1)S(1)} %collective-permute-done.3, bf16[2,128,2048]{2,1,0:T(8,128)(2,1)S(1)} %copy-done.3, s32[]{:T(128)S(6)} %min.20, pred[]{:T(512)S(6)} %eq.14), kind=kOutput, calls=%fused_computation.37 | convolution fusion | flops 537264128 | bytes 5505029 | tf_op jit(solution)/shard_map/td,rd->tr/dot_general | solution.py:55
  250.2 1.0 reduce-scatter.17.cloned.1.call-done
  251.2 1.4 bitcast_convert_fusion
  252.5 22.0 %reduce-scatter.15.cloned.1.call-done = bf16[128,256]{1,0:T(8,128)(2,1)} async-done(((bf16[128,1024]{1,0:T(8,128)(2,1)}), bf16[128,256]{1,0:T(8,128)(2,1)}) %reduce-scatter.15.cloned.1.call-update) | async-done | bytes 65552 | tf_op jit(solution)/shard_map/reduce_scatter | solution.py:58
  274.5 14.2 %all_gather.31 = bf16[128,1024]{1,0:T(8,128)(2,1)S(1)} all-gather(bf16[128,256]{1,0:T(8,128)(2,1)} %reduce-scatter.15.cloned.1.call-done), channel_id=1, replica_groups=mesh['section'=4,'dp'=2,'tensor'=4] {'tensor'}, dimensions={1}, use_global_device_ids=true | all-gather | bytes 327680 | tf_op jit(solution)/shard_map/all_gather | solution.py:61
  288.7 4.7 %fusion.56 = bf16[1,2,128,2048]{3,2,1,0:T(8,128)(2,1)} fusion(bf16[1,2,128,2048]{3,2,1,0:T(8,128)(2,1)} %copy.135, s32[]{:T(128)S(6)} %min.20, bf16[128,1024]{1,0:T(8,128)(2,1)S(1)} %all_gather.31, bf16[1,2048,1024]{2,1,0:T(8,128)(2,1)} %all-gather.8.cloned.1.call-done, f32[16,8,16,128]{3,2,1,0:T(8,128)S(1)} %bitcast.276, ...), kind=kOutput, calls=%fused_computation.32 | convolution fusion | flops 537657344 | bytes 6553605 | tf_op jit(solution)/shard_map/tr,dr->td/dot_general | solution.py:77
  (89 shorter events, 10.9 us)
Async XLA Ops:
  7.2 18.8 %all-gather.6.cloned.1.call-start = ((), (), s32[]{:S(2)}) async-start(), calls=%async_computation.12 | async-start | bytes 6291456 | tf_op jit(solution)/shard_map/all_gather | solution.py:24
  7.9 23.4 %copy-start.3 = (bf16[2,128,2048]{2,1,0:T(8,128)(2,1)S(1)}, bf16[2,128,2048]{2,1,0:T(8,128)(2,1)}, u32[]{:S(2)}) copy-start(bf16[2,128,2048]{2,1,0:T(8,128)(2,1)} %param.7) | copy-start | bytes 3145732
  7.9 44.0 %reduce-scatter.7.cloned.1.call-start = ((), (), s32[]{:S(2)}) async-start(), calls=%async_computation.6 | async-start | bytes 327680 | tf_op jit(solution)/shard_map/reduce_scatter | solution.py:58
  8.0 24.1 %copy-start.13 = (s32[1,8]{1,0:T(1,128)S(1)}, s32[1,8]{1,0:T(1,128)}, u32[]{:S(2)}) copy-start(s32[1,8]{1,0:T(1,128)} %param.12) | copy-start | bytes 100
  8.0 24.8 %copy-start.14 = (s32[1,8]{1,0:T(1,128)S(1)}, s32[1,8]{1,0:T(1,128)}, u32[]{:S(2)}) copy-start(s32[1,8]{1,0:T(1,128)} %param.13) | copy-start | bytes 100
  8.0 25.6 %copy-start.4 = (bf16[1,2,128,2048]{3,2,1,0:T(8,128)(2,1)S(1)}, bf16[1,2,128,2048]{3,2,1,0:T(8,128)(2,1)}, u32[]{:S(2)}) copy-start(bf16[1,2,128,2048]{3,2,1,0:T(8,128)(2,1)} %param.8) | copy-start | bytes 3145732
  30.5 35.3 %all-gather.8.cloned.1.call-start = ((), (), s32[]{:S(2)}) async-start(), calls=%async_computation.13 | async-start | bytes 6291456 | tf_op jit(solution)/shard_map/all_gather | solution.py:25
  31.3 79.2 %reduce-scatter.9.cloned.1.call-start = ((), (), s32[]{:S(2)}) async-start(), calls=%async_computation.7 | async-start | bytes 327680 | tf_op jit(solution)/shard_map/reduce_scatter | solution.py:58
  31.3 4.8 %copy-start.12 = (bf16[1,1,128,128]{3,2,1,0:T(8,128)(2,1)S(1)}, bf16[1,1,128,128]{3,2,1,0:T(8,128)(2,1)}, u32[]{:S(2)}) copy-start(bf16[1,1,128,128]{3,2,1,0:T(8,128)(2,1)} %param.11) | copy-start | bytes 98308
  70.7 15.7 %collective-permute-start = (bf16[128,2048]{1,0:T(8,128)(2,1)}, bf16[128,2048]{1,0:T(8,128)(2,1)S(1)}, u32[]{:S(2)}, u32[]{:S(2)}) collective-permute-start(bf16[128,2048]{1,0:T(8,128)(2,1)} %get-tuple-element.18), channel_id=1, source_target_pairs={{8,0},{16,8},{24,16},{9,1},{17,9},{25,17},{10,2},{18,10},{26,18},{... | collective-permute-start | bytes 1572872 | tf_op jit(solution)/shard_map/ppermute | solution.py:10
  77.1 9.7 %copy-start = (bf16[1,1024,2048]{2,1,0:T(8,128)(2,1)S(1)}, bf16[1,1024,2048]{2,1,0:T(8,128)(2,1)}, u32[]{:S(2)}) copy-start(bf16[1,1024,2048]{2,1,0:T(8,128)(2,1)} %all-gather.6.cloned.1.call-done) | copy-start | bytes 12582916
  89.1 73.1 %reduce-scatter.11.cloned.1.call-start = ((), (), s32[]{:S(2)}) async-start(), calls=%async_computation.8 | async-start | bytes 327680 | tf_op jit(solution)/shard_map/reduce_scatter | solution.py:58
  110.4 20.3 %copy-start.5 = (bf16[16,8,16,128]{3,2,1,0:T(8,128)(2,1)S(1)}, bf16[16,8,16,128]{3,2,1,0:T(8,128)(2,1)}, u32[]{:S(2)}) copy-start(bf16[16,8,16,128]{3,2,1,0:T(8,128)(2,1)} %copy.73) | copy-start | bytes 1572868
  129.4 11.6 %collective-permute-start.1 = (bf16[128,2048]{1,0:T(8,128)(2,1)}, bf16[128,2048]{1,0:T(8,128)(2,1)S(1)}, u32[]{:S(2)}, u32[]{:S(2)}) collective-permute-start(bf16[128,2048]{1,0:T(8,128)(2,1)} %get-tuple-element.20), channel_id=1, source_target_pairs={{8,0},{16,8},{24,16},{9,1},{17,9},{25,17},{10,2},{18,10},{26,18},{... | collective-permute-start | bytes 1572872 | tf_op jit(solution)/shard_map/ppermute | solution.py:10
  132.8 8.7 %copy-start.1 = (bf16[1,1024,2048]{2,1,0:T(8,128)(2,1)S(1)}, bf16[1,1024,2048]{2,1,0:T(8,128)(2,1)}, u32[]{:S(2)}) copy-start(bf16[1,1024,2048]{2,1,0:T(8,128)(2,1)} %all-gather.6.cloned.1.call-done) | copy-start | bytes 12582916
  143.7 70.3 %reduce-scatter.13.cloned.1.call-start = ((), (), s32[]{:S(2)}) async-start(), calls=%async_computation.9 | async-start | bytes 327680 | tf_op jit(solution)/shard_map/reduce_scatter | solution.py:58
  144.4 38.3 %copy-start.9 = (bf16[128,2,128]{2,1,0:T(2,128)(2,1)S(1)}, bf16[128,2,128]{2,1,0:T(2,128)(2,1)}, u32[]{:S(2)}) copy-start(bf16[128,2,128]{2,1,0:T(2,128)(2,1)} %fusion.81) | copy-start | bytes 196612
  181.4 11.4 %collective-permute-start.2 = (bf16[128,2048]{1,0:T(8,128)(2,1)}, bf16[128,2048]{1,0:T(8,128)(2,1)S(1)}, u32[]{:S(2)}, u32[]{:S(2)}) collective-permute-start(bf16[128,2048]{1,0:T(8,128)(2,1)} %get-tuple-element.22), channel_id=1, source_target_pairs={{8,0},{16,8},{24,16},{9,1},{17,9},{25,17},{10,2},{18,10},{26,18},{... | collective-permute-start | bytes 1572872 | tf_op jit(solution)/shard_map/ppermute | solution.py:10
  184.7 8.5 %copy-start.2 = (bf16[1,1024,2048]{2,1,0:T(8,128)(2,1)S(1)}, bf16[1,1024,2048]{2,1,0:T(8,128)(2,1)}, u32[]{:S(2)}) copy-start(bf16[1,1024,2048]{2,1,0:T(8,128)(2,1)} %all-gather.6.cloned.1.call-done) | copy-start | bytes 12582916
  195.5 55.6 %reduce-scatter.17.cloned.1.call-start = ((), (), s32[]{:S(2)}) async-start(), calls=%async_computation.11 | async-start | bytes 98304 | tf_op jit(solution)/shard_map/reduce_scatter | solution.py:101
  195.8 37.9 %copy-start.6 = (f32[2,128,128]{2,1,0:T(8,128)S(1)}, f32[2,128,128]{2,1,0:T(8,128)}, u32[]{:S(2)}) copy-start(f32[2,128,128]{2,1,0:T(8,128)} %fusion.116) | copy-start | bytes 393220
  214.0 19.7 %copy-start.8 = (bf16[128,2,128]{2,1,0:T(2,128)(2,1)S(1)}, bf16[128,2,128]{2,1,0:T(2,128)(2,1)}, u32[]{:S(2)}) copy-start(bf16[128,2,128]{2,1,0:T(2,128)(2,1)} %fusion.83) | copy-start | bytes 196612
  214.0 19.9 %copy-start.10 = (bf16[128,2,128]{2,1,0:T(2,128)(2,1)S(1)}, bf16[128,2,128]{2,1,0:T(2,128)(2,1)}, u32[]{:S(2)}) copy-start(bf16[128,2,128]{2,1,0:T(2,128)(2,1)} %fusion.85) | copy-start | bytes 196612
  214.0 20.1 %copy-start.11 = (bf16[128,2,128]{2,1,0:T(2,128)(2,1)S(1)}, bf16[128,2,128]{2,1,0:T(2,128)(2,1)}, u32[]{:S(2)}) copy-start(bf16[128,2,128]{2,1,0:T(2,128)(2,1)} %fusion.87) | copy-start | bytes 196612
  232.2 12.0 %copy-start.7 = (bf16[128,2,128]{2,1,0:T(2,128)(2,1)S(1)}, bf16[128,2,128]{2,1,0:T(2,128)(2,1)}, u32[]{:S(2)}) copy-start(bf16[128,2,128]{2,1,0:T(2,128)(2,1)} %fusion.89) | copy-start | bytes 196612
  232.3 11.5 %collective-permute-start.3 = (bf16[128,2048]{1,0:T(8,128)(2,1)S(1)}, bf16[128,2048]{1,0:T(8,128)(2,1)S(1)}, u32[]{:S(2)}, u32[]{:S(2)}) collective-permute-start(bf16[128,2048]{1,0:T(8,128)(2,1)S(1)} %get-tuple-element.24), channel_id=1, source_target_pairs={{8,0},{16,8},{24,16},{9,1},{17,9},{25,17},{10,2},{18,10},{26,18},{... | collective-permute-start | bytes 1572872 | tf_op jit(solution)/shard_map/ppermute | solution.py:10
  245.1 29.4 %reduce-scatter.15.cloned.1.call-start = ((), (), s32[]{:S(2)}) async-start(), calls=%async_computation.10 | async-start | bytes 327680 | tf_op jit(solution)/shard_map/reduce_scatter | solution.py:58
Sparse Core Ops, SparseCore 0:
  9.5 16.3 all-gather.5
  30.7 21.1 reduce-scatter.6
  53.4 11.8 all-gather.7
  89.2 21.1 reduce-scatter.8
  143.8 18.3 reduce-scatter.10
  195.6 18.3 reduce-scatter.12
  245.2 5.9 reduce-scatter.16
  253.4 21.0 reduce-scatter.14
where the time goes:
time: 301 us; the launch traced here: 300 us
  waiting for transfers between devices  140 us (47%)
  blocking collectives  72.7 us (24%)
  matrix products  51 us (17%)
  between operations  14.6 us (5%)
  local copies, waits for them, and re-layouts  12.8 us (4%)
  starting transfers between devices  5.59 us (2%)
  other arithmetic  3.35 us (1%)
    reduce_scatter x5, waiting for transfers between devices, on_device(): lax.psum_scatter(partial_value.astype(jnp.bfloat16), 'tensor', scatter_di...  91.2 us
    all_gather x5, blocking collectives, on_device(): rank_act = lax.all_gather(share, 'tensor', axis=1, tiled=True)  70.8 us
    ppermute x4, waiting for transfers between devices, shifted(): lax.ppermute(value, axis, [(source, source + steps) for source in range(i...  28.5 us
    dot_general x5, matrix products, on_device(): jnp.einsum('tr,dr->td', rank_act, right_full, preferred_element_type=jnp....  23.1 us
    all_gather x1, waiting for transfers between devices, on_device(): lax.all_gather(factor_a[0], 'dp', axis=0, tiled=True)  17.9 us
    dot_general x5, matrix products, on_device(): jnp.einsum('td,rd->tr', cot_now, left_full, preferred_element_type=jnp.fl...  15.7 us
    unnamed x43, local copies, waits for them, and re-layouts  9.95 us
  transfers between devices with their start and end apart: 12, of which 11 were waited for; matrix products, arithmetic and copies ran while one was open for 10% of the time, Pallas kernels for 0%

commit v1 on v0

v1 whole, which is shorter than its diff:
```python
import functools

import jax
import jax.numpy as jnp
from jax import lax
from jax.experimental import pallas as pl
from jax.experimental.pallas import tpu as pltpu
from jax.sharding import PartitionSpec as P

PARTS = 2
WIDE = 512
MESH = pl.DeviceIdType.MESH
NT = (((1,), (1,)), ((), ()))
TN = (((0,), (0,)), ((), ()))


def dot(lhs, rhs, dims):
    return lax.dot_general(lhs, rhs, dims, preferred_element_type=jnp.float32)


def kernel(
    dims,
    cot, stash, fa, fb, bv, rows, cols,
    out, bg,
    u, a, b, v, st, acc, psend, rsb, rk, gs, sp, gacc, gsend, grecv,
    a_sem, b_sem, v_sem, st_sem, u_sem, us_sem, rs_sem, rr_sem, as_sem, ar_sem, o_sem, g_sem,
):
    sections, dp, tensor, paired = dims
    sec = lax.axis_index("section")
    dpi = lax.axis_index("dp")
    me = lax.axis_index("tensor")
    chunks, pieces, chunk, wide = u.shape
    bs = v.shape[-1]
    per = wide // bs
    local_blocks = pieces * per
    nblocks = v.shape[0]
    blk = nblocks // dp
    last = sections - 1

    barrier = pltpu.get_barrier_semaphore()

    def greet(axis, index):
        pl.semaphore_signal(barrier, inc=1, device_id={axis: index}, device_id_type=MESH)

    greet("section", lax.rem(sec + 1, sections))
    greet("section", lax.rem(sec + sections - 1, sections))
    for off in range(1, tensor):
        greet("tensor", lax.rem(me + off, tensor))
    if paired:
        greet("dp", 1 - dpi)

    def cot_copy(c, j):
        return pltpu.make_async_copy(
            cot.at[c, :, pl.ds(j * wide, wide)], u.at[c, j], u_sem.at[c, j]
        )

    @pl.when(sec == last)
    def _():
        def go(c, _):
            for j in range(pieces):
                cot_copy(c, j).start()
            return 0

        lax.fori_loop(0, chunks, go, 0)

    def share(src, dst, sem):
        if not paired:
            return [pltpu.make_async_copy(src, dst, sem.at[0])], None, None
        size = src.shape[0]
        mine = dst.at[pl.ds(dpi * size, size)]
        other = dst.at[pl.ds((1 - dpi) * size, size)]
        local = pltpu.make_async_copy(src, mine, sem.at[0])
        push = pltpu.make_async_remote_copy(
            src, mine, sem.at[1], sem.at[2], device_id={"dp": 1 - dpi}, device_id_type=MESH
        )
        pull = pltpu.make_async_remote_copy(
            src, other, sem.at[1], sem.at[2], device_id={"dp": 1 - dpi}, device_id_type=MESH
        )
        return [local], push, pull

    a_copy, b_copy, v_copy = share(fa, a, a_sem), share(fb, b, b_sem), share(bv, v, v_sem)
    st_copy = pltpu.make_async_copy(stash, st, st_sem)
    a_copy[0][0].start()
    pl.semaphore_wait(barrier, 2 + (tensor - 1) + (1 if paired else 0))
    if paired:
        a_copy[1].start()
    for one in (v_copy, b_copy):
        one[0][0].start()
        if paired:
            one[1].start()
    st_copy.start()
    gacc[...] = jnp.zeros_like(gacc)

    def arrive(one):
        one[0][0].wait()
        if paired:
            one[2].wait_recv()

    def rs_copy(c, src, k):
        return pltpu.make_async_remote_copy(
            psend.at[c, k], rsb.at[c, src], rs_sem.at[c, k], rr_sem.at[c, src],
            device_id={"tensor": k}, device_id_type=MESH,
        )

    def ag_copy(c, src, k):
        return pltpu.make_async_remote_copy(
            rk.at[c, src], rk.at[c, src], as_sem.at[c, k], ar_sem.at[c, src],
            device_id={"tensor": k}, device_id_type=MESH,
        )

    def hop_copy(c, j):
        return pltpu.make_async_remote_copy(
            gs.at[c, j], u.at[c, j], us_sem.at[c, j], u_sem.at[c, j],
            device_id={"section": lax.rem(sec + sections - 1, sections)}, device_id_type=MESH,
        )

    def out_copy(c, j):
        return pltpu.make_async_copy(
            gs.at[c, j], out.at[c, :, pl.ds(j * wide, wide)], o_sem.at[c, j]
        )

    def place(n):
        return (n // blk * tensor + me) * blk + n % blk

    def project(c):
        for j in range(pieces):

            @pl.when(sec == last)
            def _():
                cot_copy(c, j).wait()

            @pl.when(sec != last)
            def _():
                hop_copy(c, j).wait_recv()

            piece = u[c, j]
            span = acc.shape[-1]
            for k in range(tensor):
                term = dot(piece, a[k * span : (k + 1) * span, j * wide : (j + 1) * wide], NT)
                if j > 0:
                    term = acc[k] + term
                acc[k] = term
                if j == pieces - 1:
                    psend[c, k] = term.astype(jnp.bfloat16)

                    @pl.when(me != k)
                    def _():
                        rs_copy(c, me, k).start()

    def sparse(c):
        def one(n, _):
            row = rows[0, place(n)] - me * local_blocks
            col = cols[0, place(n)] - me * local_blocks
            rows_at = jnp.full((chunk, bs), row, jnp.int32)
            cols_at = jnp.full((chunk, bs), col, jnp.int32)
            picked = jnp.zeros((chunk, bs), jnp.float32)
            inner = jnp.zeros((chunk, bs), jnp.float32)
            for at in range(local_blocks):
                here = at % per * bs
                seen = u[c, at // per, :, here : here + bs].astype(jnp.float32)
                picked = jnp.where(cols_at == at, seen, picked)
                held = st[c, :, at * bs : (at + 1) * bs].astype(jnp.float32)
                inner = jnp.where(rows_at == at, held, inner)
            picked = picked.astype(jnp.bfloat16)
            sp[c, n] = dot(picked, v[n], NT)
            gacc[n] += dot(inner.astype(jnp.bfloat16), picked, TN)
            return 0

        lax.fori_loop(0, nblocks, one, 0, unroll=nblocks <= 4)

    def reduce(c):
        total = acc[me]
        for off in range(1, tensor):
            src = lax.rem(me + off, tensor)
            rs_copy(c, src, src).wait_recv()
            total = total + rsb[c, src].astype(jnp.float32)
        rk[c, me] = total.astype(jnp.bfloat16)
        for off in range(1, tensor):
            ag_copy(c, me, lax.rem(me + off, tensor)).start()

    def expand(c):
        for off in range(1, tensor):
            src = lax.rem(me + off, tensor)
            ag_copy(c, src, src).wait_recv()
        rank = jnp.concatenate([rk[c, k] for k in range(tensor)], axis=1)
        lane = lax.broadcasted_iota(jnp.int32, (chunk, wide), 1) // bs
        for j in range(pieces):
            dense = dot(rank, b[j * wide : (j + 1) * wide, :], NT)

            def one(n, total):
                row = rows[0, place(n)] - me * local_blocks - j * per
                tiled = jnp.concatenate([sp[c, n]] * per, axis=1)
                return total + jnp.where(lane == row, tiled, 0.0)

            total = lax.fori_loop(0, nblocks, one, jnp.zeros_like(dense), unroll=nblocks <= 4)
            gs[c, j] = (dense + total).astype(jnp.bfloat16)

            @pl.when(sec > 0)
            def _():
                hop_copy(c, j).start()

            out_copy(c, j).start()

    arrive(a_copy)

    def step(i, _):
        @pl.when(i < chunks)
        def _():
            project(i)

            @pl.when(i == 0)
            def _():
                arrive(v_copy)
                st_copy.wait()

            sparse(i)

        @pl.when(i == 1)
        def _():
            arrive(b_copy)

        @pl.when(i > 0)
        def _():
            expand(i - 1)

        @pl.when(i < chunks)
        def _():
            reduce(i)

        return 0

    lax.fori_loop(0, chunks + 1, step, 0)

    if paired:
        gsend[...] = gacc[pl.ds((1 - dpi) * blk, blk)].astype(jnp.bfloat16)
        swap = pltpu.make_async_remote_copy(
            gsend, grecv, g_sem.at[0], g_sem.at[1], device_id={"dp": 1 - dpi}, device_id_type=MESH
        )
        swap.start()
    else:
        bg[...] = gacc[...].astype(bg.dtype)

    def drain(c, _):
        for off in range(1, tensor):
            dst = lax.rem(me + off, tensor)
            rs_copy(c, me, dst).wait_send()
            ag_copy(c, me, dst).wait_send()
        for j in range(pieces):

            @pl.when(sec > 0)
            def _():
                hop_copy(c, j).wait_send()

            out_copy(c, j).wait()
        return 0

    lax.fori_loop(0, chunks, drain, 0)
    if paired:
        for one in (a_copy, v_copy, b_copy):
            one[1].wait_send()
        swap.wait()
        kept = gacc[pl.ds(dpi * blk, blk)].astype(jnp.bfloat16).astype(jnp.float32)
        bg[...] = kept + grecv[...].astype(jnp.float32)


def on_device(cotangent, stash, factor_a, factor_b, block_vals, block_rows, block_cols):
    sections = lax.axis_size("section")
    dp = lax.axis_size("dp")
    tensor = lax.axis_size("tensor")
    paired = dp == 2
    _, batches, tokens, width = stash.shape
    rank = factor_b.shape[-1]
    blk, bs = block_vals.shape[1:3]
    parts = [factor_a[0], factor_b[0], block_vals[0]]
    if not paired:
        parts = [lax.all_gather(part, "dp", axis=0, tiled=True) for part in parts]
    nblocks = dp * blk
    chunks, chunk = batches * PARTS, tokens // PARTS
    wide = min(WIDE, width)
    pieces = width // wide
    span = rank // tensor
    bf, f32 = jnp.bfloat16, jnp.float32
    vmem, dma = pltpu.VMEM, pltpu.SemaphoreType.DMA
    hbm = pl.BlockSpec(memory_space=pl.ANY)
    smem = pl.BlockSpec(memory_space=pltpu.SMEM)
    grads, blocks = pl.pallas_call(
        functools.partial(kernel, (sections, dp, tensor, paired)),
        out_shape=(
            jax.ShapeDtypeStruct((chunks, chunk, width), bf),
            jax.ShapeDtypeStruct((blk if paired else nblocks, bs, bs), f32 if paired else bf),
        ),
        in_specs=[hbm] * 5 + [smem] * 2,
        out_specs=(hbm, pl.BlockSpec(memory_space=vmem)),
        scratch_shapes=[
            vmem((chunks, pieces, chunk, wide), bf),
            vmem((rank, width), bf),
            vmem((width, rank), bf),
            vmem((nblocks, bs, bs), bf),
            vmem((chunks, chunk, width), bf),
            vmem((tensor, chunk, span), f32),
            vmem((chunks, tensor, chunk, span), bf),
            vmem((chunks, tensor, chunk, span), bf),
            vmem((chunks, tensor, chunk, span), bf),
            vmem((chunks, pieces, chunk, wide), bf),
            vmem((chunks, nblocks, chunk, bs), f32),
            vmem((nblocks, bs, bs), f32),
            vmem((blk, bs, bs), bf),
            vmem((blk, bs, bs), bf),
            dma((3,)),
            dma((3,)),
            dma((3,)),
            dma,
            dma((chunks, pieces)),
            dma((chunks, pieces)),
            dma((chunks, tensor)),
            dma((chunks, tensor)),
            dma((chunks, tensor)),
            dma((chunks, tensor)),
            dma((chunks, pieces)),
            dma((2,)),
        ],
        compiler_params=pltpu.CompilerParams(
            collective_id=0, has_side_effects=True, vmem_limit_bytes=48 << 20
        ),
    )(
        cotangent.reshape(chunks, chunk, width),
        stash.reshape(chunks, chunk, width),
        *parts,
        block_rows,
        block_cols,
    )
    if not paired:
        blocks = lax.psum_scatter(blocks, "dp", scatter_dimension=0, tiled=True).astype(f32)
    return grads.reshape(stash.shape), blocks[None]


def solution(mesh):
    in_specs = (
        P(None, "dp", "tensor"),
        P("section", None, "dp", "tensor"),
        P("section", "dp", "tensor"),
        P("section", ("tensor", "dp"), None),
        P("section", ("dp", "tensor"), None, None),
        P("section", None),
        P("section", None),
    )
    out_specs = (P("section", None, "dp", "tensor"), P("section", ("dp", "tensor"), None, None))
    return jax.shard_map(
        on_device, mesh=mesh, in_specs=in_specs, out_specs=out_specs, check_vma=False
    )
```

time: 301 us -> 105 us (0.35)
  waiting for transfers between devices: 140 us -> 0 us
  Pallas kernels: 0 us -> 96.8 us
  blocking collectives: 72.7 us -> 0 us
  matrix products: 51 us -> 0 us
  between operations: 14.6 us -> 0.65 us
  starting transfers between devices: 5.59 us -> 0 us
  local copies, waits for them, and re-layouts: 12.8 us -> 7.7 us
  other arithmetic: 3.35 us -> 0 us
    pallas_call x0 -> x1, Pallas kernels: none -> 96.8 us  [on_device(): pl.pallas_call(functools.partial(kernel, (sections, dp, tensor, paired)),...]
    reduce_scatter x6 -> x0, waiting for transfers between devices: 92.2 us -> none  [the longest x5 91.2 us: on_device(): lax.psum_scatter(partial_value.astype(jnp.bfloat16), 'tensor', scatter_di...]
    all_gather x6 -> x0, blocking collectives: 72.7 us -> none  [the longest x5 70.8 us: on_device(): rank_act = lax.all_gather(share, 'tensor', axis=1, tiled=True)]
    dot_general x35 -> x0, matrix products: 51 us -> none  [the longest x5 23.1 us: on_device(): jnp.einsum('tr,dr->td', rank_act, right_full, preferred_element_type=jnp....]
    ppermute x4 -> x0, waiting for transfers between devices: 28.5 us -> none  [shifted(): lax.ppermute(value, axis, [(source, source + steps) for source in range(i...]
    all_gather x2 -> x0, waiting for transfers between devices: 17.9 us -> none  [the longest x1 17.9 us: on_device(): lax.all_gather(factor_a[0], 'dp', axis=0, tiled=True)]
    ppermute x4 -> x0, starting transfers between devices: 5.26 us -> none  [shifted(): lax.ppermute(value, axis, [(source, source + steps) for source in range(i...]
    unnamed x43 -> x14, local copies, waits for them, and re-layouts: 9.95 us -> 7.7 us
  transfers between devices with their start and end apart: 12 -> 0, of which waited for: 11 -> 0; matrix products, arithmetic and copies ran while one was open for 10% -> 0% of each run, Pallas kernels for 0% -> 0%
where the time goes in v1:
time: 105 us
  Pallas kernels  96.8 us (92%)
  local copies, waits for them, and re-layouts  7.7 us (7%)
    pallas_call x1, Pallas kernels, on_device(): pl.pallas_call(functools.partial(kernel, (sections, dp, tensor, paired)),...  96.8 us
    unnamed x14, local copies, waits for them, and re-layouts  7.7 us

profile of v1, /device:TPU:0, one launch (start us, length us, event | category | flops | bytes accessed | tf_op | source)
XLA Modules:
  0.0 105.2 jit_solution(5457513350202754866)
XLA Ops:
  0.6 0.0 copy-start
  0.6 1.6 %copy-done = bf16[1,512,2048]{2,1,0:T(8,128)(2,1)S(1)} copy-done((bf16[1,512,2048]{2,1,0:T(8,128)(2,1)S(1)}, bf16[1,512,2048]{2,1,0:T(8,128)(2,1)}, u32[]{:S(2)}) %copy-start) | copy-done | bytes 2097176
  2.2 0.0 copy-start.1
  2.2 1.2 %copy-done.1 = bf16[2,128,2048]{2,1,0:T(8,128)(2,1)S(1)} copy-done((bf16[2,128,2048]{2,1,0:T(8,128)(2,1)S(1)}, bf16[2,128,2048]{2,1,0:T(8,128)(2,1)}, u32[]{:S(2)}) %copy-start.1) | copy-done | bytes 1048600
  3.4 0.0 copy-start.2
  3.5 1.2 %copy-done.2 = bf16[1,2,128,2048]{3,2,1,0:T(8,128)(2,1)S(1)} copy-done((bf16[1,2,128,2048]{3,2,1,0:T(8,128)(2,1)S(1)}, bf16[1,2,128,2048]{3,2,1,0:T(8,128)(2,1)}, u32[]{:S(2)}) %copy-start.2) | copy-done | bytes 1048600
  4.7 0.0 copy-start.3
  4.7 0.8 copy-done.3
  5.4 0.0 copy-start.4
  5.4 0.7 copy-done.4
  6.1 0.0 copy-start.5
  6.1 0.7 copy-done.5
  6.7 96.8 %shard_map.86 = (bf16[4,64,2048]{2,1,0:T(8,128)(2,1)S(1)}, f32[1,128,128]{2,1,0:T(8,128)S(1)}) custom-call(bf16[4,64,2048]{2,1,0:T(8,128)(2,1)S(1)} %bitcast.9, bf16[4,64,2048]{2,1,0:T(8,128)(2,1)S(1)} %bitcast.10, bf16[512,2048]{1,0:T(8,128)(2,1)S(1)} %bitcast.7, bf16[1024,1024]{1,0:T(8,128)(2,1)} %bitcast.13, bf16[1,128,128]{2,1,0:T(8,128)(2,1)S(1)} %bitcast.12, ...), custom_call_target="tpu_custom_call" | custom-call | tf_op jit(solution)/shard_map/pallas_call | solution.py:286
  103.6 1.0 copy.11
  104.5 0.6 copy.12
Async XLA Ops:
  0.6 1.6 %copy-start = (bf16[1,512,2048]{2,1,0:T(8,128)(2,1)S(1)}, bf16[1,512,2048]{2,1,0:T(8,128)(2,1)}, u32[]{:S(2)}) copy-start(bf16[1,512,2048]{2,1,0:T(8,128)(2,1)} %param.9) | copy-start | bytes 6291460
  2.2 1.2 %copy-start.1 = (bf16[2,128,2048]{2,1,0:T(8,128)(2,1)S(1)}, bf16[2,128,2048]{2,1,0:T(8,128)(2,1)}, u32[]{:S(2)}) copy-start(bf16[2,128,2048]{2,1,0:T(8,128)(2,1)} %param.7) | copy-start | bytes 3145732
  3.4 1.2 %copy-start.2 = (bf16[1,2,128,2048]{3,2,1,0:T(8,128)(2,1)S(1)}, bf16[1,2,128,2048]{3,2,1,0:T(8,128)(2,1)}, u32[]{:S(2)}) copy-start(bf16[1,2,128,2048]{3,2,1,0:T(8,128)(2,1)} %param.8) | copy-start | bytes 3145732
  4.7 0.8 copy-start.3
  5.4 0.7 copy-start.4
  6.1 0.7 copy-start.5

commit v2 on v1

--- a/solution.py
+++ b/solution.py
@@ -7,10 +7,13 @@
 from jax.experimental.pallas import tpu as pltpu
 from jax.sharding import PartitionSpec as P
 
-PARTS = 2
+PARTS = 4
+SUM_LAG = 1
+OUT_LAG = 2
 WIDE = 512
 MESH = pl.DeviceIdType.MESH
 NT = (((1,), (1,)), ((), ()))
+NN = (((1,), (0,)), ((), ()))
 TN = (((0,), (0,)), ((), ()))
 
 
@@ -22,7 +25,7 @@
     dims,
     cot, stash, fa, fb, bv, rows, cols,
     out, bg,
-    u, a, b, v, st, acc, psend, rsb, rk, gs, sp, gacc, gsend, grecv,
+    u, a, b, at, bt, v, st, acc, psend, rsb, rk, gs, sp, gacc, gsend, grecv,
     a_sem, b_sem, v_sem, st_sem, u_sem, us_sem, rs_sem, rr_sem, as_sem, ar_sem, o_sem, g_sem,
 ):
     sections, dp, tensor, paired = dims
@@ -84,10 +87,9 @@
     pl.semaphore_wait(barrier, 2 + (tensor - 1) + (1 if paired else 0))
     if paired:
         a_copy[1].start()
-    for one in (v_copy, b_copy):
-        one[0][0].start()
-        if paired:
-            one[1].start()
+    v_copy[0][0].start()
+    if paired:
+        v_copy[1].start()
     st_copy.start()
     gacc[...] = jnp.zeros_like(gacc)
 
@@ -122,24 +124,23 @@
     def place(n):
         return (n // blk * tensor + me) * blk + n % blk
 
-    def project(c):
+    def project(c, turned):
         for j in range(pieces):
-
-            @pl.when(sec == last)
-            def _():
+            if turned:
+                hop_copy(c, j).wait_recv()
+            else:
                 cot_copy(c, j).wait()
-
-            @pl.when(sec != last)
-            def _():
-                hop_copy(c, j).wait_recv()
-
             piece = u[c, j]
             span = acc.shape[-1]
             for k in range(tensor):
-                term = dot(piece, a[k * span : (k + 1) * span, j * wide : (j + 1) * wide], NT)
+                ranks, columns = pl.ds(k * span, span), pl.ds(j * wide, wide)
+                if turned:
+                    term = dot(piece, at[columns, ranks], NN)
+                else:
+                    term = dot(piece, a[ranks, columns], NT)
                 if j > 0:
-                    term = acc[k] + term
-                acc[k] = term
+                    term = acc[c % acc.shape[0], k] + term
+                acc[c % acc.shape[0], k] = term
                 if j == pieces - 1:
                     psend[c, k] = term.astype(jnp.bfloat16)
 
@@ -169,7 +170,7 @@
         lax.fori_loop(0, nblocks, one, 0, unroll=nblocks <= 4)
 
     def reduce(c):
-        total = acc[me]
+        total = acc[c % acc.shape[0], me]
         for off in range(1, tensor):
             src = lax.rem(me + off, tensor)
             rs_copy(c, src, src).wait_recv()
@@ -178,14 +179,17 @@
         for off in range(1, tensor):
             ag_copy(c, me, lax.rem(me + off, tensor)).start()
 
-    def expand(c):
+    def expand(c, turned):
         for off in range(1, tensor):
             src = lax.rem(me + off, tensor)
             ag_copy(c, src, src).wait_recv()
         rank = jnp.concatenate([rk[c, k] for k in range(tensor)], axis=1)
         lane = lax.broadcasted_iota(jnp.int32, (chunk, wide), 1) // bs
         for j in range(pieces):
-            dense = dot(rank, b[j * wide : (j + 1) * wide, :], NT)
+            if turned:
+                dense = dot(rank, bt[:, j * wide : (j + 1) * wide], NN)
+            else:
+                dense = dot(rank, b[j * wide : (j + 1) * wide, :], NT)
 
             def one(n, total):
                 row = rows[0, place(n)] - me * local_blocks - j * per
@@ -195,19 +199,58 @@
             total = lax.fori_loop(0, nblocks, one, jnp.zeros_like(dense), unroll=nblocks <= 4)
             gs[c, j] = (dense + total).astype(jnp.bfloat16)
 
-            @pl.when(sec > 0)
-            def _():
+            if turned:
+
+                @pl.when(sec > 0)
+                def _():
+                    hop_copy(c, j).start()
+
+            else:
                 hop_copy(c, j).start()
 
             out_copy(c, j).start()
 
     arrive(a_copy)
+    b_copy[0][0].start()
+    if paired:
+        b_copy[1].start()
+
+    @pl.when(sec != last)
+    def _():
+        def turn(src, dst):
+            height, length = src.shape
+            tile = min(height, length, 256)
+
+            def go(n, _):
+                top = pl.multiple_of(n * tile, tile)
+                for x in range(0, length, tile):
+                    dst[x : x + tile, pl.ds(top, tile)] = src[pl.ds(top, tile), x : x + tile].T
+                return 0
+
+            lax.fori_loop(0, height // tile, go, 0)
+
+        turn(a, at)
+        arrive(b_copy)
+        turn(b, bt)
 
     def step(i, _):
         @pl.when(i < chunks)
         def _():
-            project(i)
-
+            @pl.when(sec == last)
+            def _():
+                project(i, False)
+
+            @pl.when(sec != last)
+            def _():
+                project(i, True)
+
+
+        @pl.when((i >= SUM_LAG) & (i < chunks + SUM_LAG))
+        def _():
+            reduce(i - SUM_LAG)
+
+        @pl.when(i < chunks)
+        def _():
             @pl.when(i == 0)
             def _():
                 arrive(v_copy)
@@ -215,21 +258,21 @@
 
             sparse(i)
 
-        @pl.when(i == 1)
-        def _():
-            arrive(b_copy)
-
-        @pl.when(i > 0)
-        def _():
-            expand(i - 1)
-
-        @pl.when(i < chunks)
-        def _():
-            reduce(i)
+        @pl.when((i >= OUT_LAG) & (sec == last))
+        def _():
+            @pl.when(i == OUT_LAG)
+            def _():
+                arrive(b_copy)
+
+            expand(i - OUT_LAG, False)
+
+        @pl.when((i >= OUT_LAG) & (sec != last))
+        def _():
+            expand(i - OUT_LAG, True)
 
         return 0
 
-    lax.fori_loop(0, chunks + 1, step, 0)
+    lax.fori_loop(0, chunks + OUT_LAG, step, 0)
 
     if paired:
         gsend[...] = gacc[pl.ds((1 - dpi) * blk, blk)].astype(jnp.bfloat16)
@@ -281,7 +324,7 @@
     span = rank // tensor
     bf, f32 = jnp.bfloat16, jnp.float32
     vmem, dma = pltpu.VMEM, pltpu.SemaphoreType.DMA
-    hbm = pl.BlockSpec(memory_space=pl.ANY)
+    hbm = pl.BlockSpec(memory_space=pltpu.HBM)
     smem = pl.BlockSpec(memory_space=pltpu.SMEM)
     grads, blocks = pl.pallas_call(
         functools.partial(kernel, (sections, dp, tensor, paired)),
@@ -295,9 +338,11 @@
             vmem((chunks, pieces, chunk, wide), bf),
             vmem((rank, width), bf),
             vmem((width, rank), bf),
+            vmem((width, rank), bf),
+            vmem((rank, width), bf),
             vmem((nblocks, bs, bs), bf),
             vmem((chunks, chunk, width), bf),
-            vmem((tensor, chunk, span), f32),
+            vmem((SUM_LAG + 1, tensor, chunk, span), f32),
             vmem((chunks, tensor, chunk, span), bf),
             vmem((chunks, tensor, chunk, span), bf),
             vmem((chunks, tensor, chunk, span), bf),
@@ -320,7 +365,7 @@
             dma((2,)),
         ],
         compiler_params=pltpu.CompilerParams(
-            collective_id=0, has_side_effects=True, vmem_limit_bytes=48 << 20
+            collective_id=0, has_side_effects=True, vmem_limit_bytes=60 << 20
         ),
     )(
         cotangent.reshape(chunks, chunk, width),

time: 105 us -> 97.7 us (0.930)
  local copies, waits for them, and re-layouts: 7.7 us -> 2.97 us
  Pallas kernels: 96.8 us -> 93.9 us
    unnamed x14 -> x4, local copies, waits for them, and re-layouts: 7.7 us -> 2.97 us
    pallas_call x1, Pallas kernels: 96.8 us -> 93.9 us  [on_device(): pl.pallas_call(functools.partial(kernel, (sections, dp, tensor, paired)),...]
where the time goes in v2:
time: 97.7 us; the launch traced here: 97.5 us
  Pallas kernels  93.9 us (96%)
  local copies, waits for them, and re-layouts  2.97 us (3%)
    pallas_call x1, Pallas kernels, on_device(): pl.pallas_call(functools.partial(kernel, (sections, dp, tensor, paired)),...  93.9 us
    unnamed x4, local copies, waits for them, and re-layouts  2.97 us

profile of v2, /device:TPU:0, one launch (start us, length us, event | category | flops | bytes accessed | tf_op | source)
XLA Modules:
  0.0 97.5 jit_solution(1887040876182885968)
XLA Ops:
  0.6 93.9 %shard_map.86 = (bf16[8,32,2048]{2,1,0:T(8,128)(2,1)}, f32[1,128,128]{2,1,0:T(8,128)}) custom-call(bf16[8,32,2048]{2,1,0:T(8,128)(2,1)} %bitcast.10, bf16[8,32,2048]{2,1,0:T(8,128)(2,1)} %bitcast.11, bf16[512,2048]{1,0:T(8,128)(2,1)} %bitcast.7, bf16[1024,1024]{1,0:T(8,128)(2,1)} %bitcast.8, bf16[1,128,128]{2,1,0:T(8,128)(2,1)} %bitcast.13, s32[1,8]{1,0:T(1,128)} %rows.1, ...), custom_call_target="tpu_custom_call" | custom-call | tf_op jit(solution)/shard_map/pallas_call | solution.py:329
  94.6 0.0 copy-start
  94.6 2.3 %copy.11 = bf16[1,2,128,2048]{3,2,1,0:T(8,128)(2,1)} copy(bf16[1,2,128,2048]{3,2,1,0:T(8,128)(2,1)} %bitcast.9) | data formatting | bytes 2097152
  96.9 0.0 copy-done
  96.9 0.6 copy.12
Async XLA Ops:
  94.6 2.3 %copy-start = (f32[1,128,128]{2,1,0:T(8,128)S(1)}, f32[1,128,128]{2,1,0:T(8,128)}, u32[]{:S(2)}) copy-start(f32[1,128,128]{2,1,0:T(8,128)} %get-tuple-element.5) | copy-start | bytes 196612
